TPU v7x, 32 devices: a whole 2x2x4 slice. The times are simulated.
32 devices in a mesh: groups: 2 (over y), tm: 4 (over z), fsdp: 4 (over x, core).
Axes of the slice: x: 2, y: 2, z: 4, core: 2. Of those that a mesh axis runs over, the one named last changes fastest.
Arguments:
- query_proj: bfloat16 [8192, 1024], P(('groups', 'tm'), 'fsdp'), parts along dimension 0, may hold values from -0.75 to 0.75
- key_proj: bfloat16 [8192, 1024], P(('groups', 'tm'), 'fsdp'), parts along dimension 0, may hold values from -0.75 to 0.75
- value_proj: bfloat16 [8192, 1024], P(('groups', 'tm'), 'fsdp'), parts along dimension 0, may hold values from -6 to 6
- log_decay: float32 [8192, 16], P(('groups', 'tm'), 'fsdp'), parts along dimension 0, may hold values from -0.5 to 0, as said below
- out_grad: bfloat16 [8192, 1024], P(('groups', 'tm'), 'fsdp'), parts along dimension 0, may hold values from -6 to 6
- out_weight: bfloat16 [1024, 1024], P('fsdp', 'tm'), may hold values from -0.1875 to 0.1875
Outputs:
- query_grad: bfloat16 [8192, 1024], P(('groups', 'tm'), 'fsdp'), parts along dimension 0
- key_grad: bfloat16 [8192, 1024], P(('groups', 'tm'), 'fsdp'), parts along dimension 0
- value_grad: bfloat16 [8192, 1024], P(('groups', 'tm'), 'fsdp'), parts along dimension 0
- decay_grad: float32 [8192, 16], P(('groups', 'tm'), 'fsdp'), parts along dimension 0
- weight_grad: float32 [2048, 1024], P(('groups', 'fsdp'), 'tm'), parts along dimension 0
There are 2 independent parts, one for each index of `groups`. A program takes and returns all parts, laid end to end along the dimension named above; an argument that names none is the same for every part. Nothing has to cross between parts.
Inputs may be any that keep to these rules, and one draw needn't show every extreme that they name: `log_decay`: each entry is the logarithm of one head's decay at one token.
All inputs are finite; a program needn't handle non-finite values.
Results may differ from a plain program's by a relative error of at most 0.0029.
Values may be sent and summed in bfloat16 or wider, within the bound.
No kernel may reach another device: no remote copies, remote signals or barrier semaphores. Data moves between devices by JAX's collectives and lax.ppermute only.
A program may use at most 128 MiB of HBM per device.

v0:
```python
import functools

import jax
import jax.numpy as jnp
from jax import lax
from jax.experimental import pallas as pl
from jax.experimental.pallas import tpu as pltpu
from jax.sharding import PartitionSpec as P


HEAD_DIM = 64
BLOCK = 128
PAD = 8
PAIR = 2 * HEAD_DIM
LOG2_E = 1.4426950408889634

F32 = jnp.float32
BF16 = jnp.bfloat16
NN = (((1,), (0,)), ((), ()))
NT = (((1,), (1,)), ((), ()))

PIECES = 2
GRANT = 24 << 20
COST = {
    "summary": 3, "inside": 4, "outputs": 3, "weight": 2, "inner": 3, "queries": 4, "sources": 4,
    "final": 4,
}


def mm(a, b, dims=NN):
    return lax.dot_general(a, b, dims, preferred_element_type=F32)


def split2(x):
    high = x.astype(BF16)
    return high, (x - high.astype(F32)).astype(BF16)


def split3(x):
    high = x.astype(BF16)
    rest = x - high.astype(F32)
    mid = rest.astype(BF16)
    return high, mid, (rest - mid.astype(F32)).astype(BF16)


def iota(shape, axis):
    return lax.broadcasted_iota(jnp.int32, shape, axis)


def ones_where(keep):
    return jnp.where(keep, 1.0, 0.0).astype(BF16)


def cat(parts, axis):
    return jnp.concatenate(parts, axis=axis)


def rows_of(b):
    return pl.ds(b * BLOCK, BLOCK)


def loop(blocks, step, carry):
    for b in range(blocks):
        carry = step(b, carry)
    return carry


def lanes_of(p):
    return slice(p * PAIR, (p + 1) * PAIR)


def first_head(like):
    return iota(like.shape, 1) < HEAD_DIM


def stacked(pair):
    keep, zero = first_head(pair), jnp.zeros_like(pair)
    return cat([jnp.where(keep, pair, zero), jnp.where(keep, zero, pair)], 0)


def spread_heads(both):
    count = both.shape[1] // PAIR
    zero = jnp.zeros((2 * both.shape[0], PAIR), both.dtype)
    out = []
    for p in range(count):
        row = [zero] * count
        row[p] = stacked(both[:, lanes_of(p)])
        out.append(cat(row, 1))
    return cat(out, 0)


def apart(pair_t):
    top, low = pair_t[:HEAD_DIM, :], pair_t[HEAD_DIM:, :]
    zero = jnp.zeros_like(top)
    return cat([cat([top, zero], 1), cat([zero, low], 1)], 0)


def turned(full):
    count = full.shape[1] // PAIR
    zero = jnp.zeros((PAIR, PAIR), full.dtype)
    out = []
    for p in range(count):
        row = [zero] * count
        row[p] = full[lanes_of(p), lanes_of(p)].T
        out.append(cat(row, 1))
    return cat(out, 0)


def compact(full):
    out = []
    for p in range(full.shape[1] // PAIR):
        mine = full[lanes_of(p), lanes_of(p)]
        top = mine[:HEAD_DIM, :]
        out.append(jnp.where(first_head(top), top, mine[HEAD_DIM:, :]))
    return cat(out, 1)


def columns_of(by_token, b):
    return by_token[:, b * PAD : (b + 1) * PAD]


def wide_all(columns, heads):
    return cat([wide_of(columns, p) for p in range(heads // 2)], 1)


def wide_of(columns, p):
    one, two = columns[:, 2 * p : 2 * p + 1], columns[:, 2 * p + 1 : 2 * p + 2]
    keep = iota((BLOCK, PAIR), 1) < HEAD_DIM
    return jnp.where(
        keep, jnp.broadcast_to(one, (BLOCK, PAIR)), jnp.broadcast_to(two, (BLOCK, PAIR))
    )


def exponents(columns, crow_block, p):
    return [
        jnp.broadcast_to(columns[:, h : h + 1], (BLOCK, BLOCK)) - crow_block[h : h + 1, :]
        for h in (2 * p, 2 * p + 1)
    ]


def pair_weights(expos, flipped):
    row, col = iota((BLOCK, BLOCK), 0), iota((BLOCK, BLOCK), 1)
    keep = (row <= col) if flipped else (row >= col)
    return cat([jnp.where(keep, jnp.exp2(-e if flipped else e), 0.0) for e in expos], 1)


def fold(both):
    half = both.shape[0] // 2
    return both[:half, :] + both[half:, :]


def wide_state(state):
    high, low = split2(state)
    return spread_heads(high), spread_heads(low)


def takes_from(mask, ahead):
    later = (lax.axis_index("tm") & mask) != 0
    return later if ahead else jnp.logical_not(later)


def entering(takes, inside, other):
    state, total = inside[:HEAD_DIM, :], inside[HEAD_DIM : HEAD_DIM + 1, :]
    return jnp.where(takes, state + jnp.exp2(total) * other[:HEAD_DIM, :], state)


def summary_kernel(
    heads, blocks, decay_far, key_far, value_far, crow, ccol, state_blocks, message,
    decay, key, value, decay_sem, sems,
):
    lanes = heads * HEAD_DIM
    first = pltpu.make_async_copy(decay_far, decay, decay_sem)
    first.start()
    copies = []
    size = key.shape[0] // PIECES
    for i in range(PIECES):
        rows = pl.ds(i * size, size)
        pair = (
            pltpu.make_async_copy(key_far.at[rows, :], key.at[rows, :], sems.at[0, i]),
            pltpu.make_async_copy(value_far.at[rows, :], value.at[rows, :], sems.at[1, i]),
        )
        for copy in pair:
            copy.start()
        copies.append(pair)
    first.wait()
    upper = ones_where(iota((BLOCK, BLOCK), 0) <= iota((BLOCK, BLOCK), 1))
    filler = [jnp.zeros((PAD - heads, BLOCK), F32)] if heads < PAD else []
    rates = cat([cat([decay[:, rows_of(b)]] + filler, 0) for b in range(blocks)], 0) * LOG2_E
    sums = mm(cat(split3(rates), 0), upper)
    size = blocks * PAD
    cum = sums[:size, :] + sums[size : 2 * size, :] + sums[2 * size :, :]
    by_token = cum.T
    ccol[...] = by_token
    state, total = jnp.zeros((HEAD_DIM, lanes), F32), jnp.zeros((1, lanes), F32)
    for b in range(blocks):
        rows = rows_of(b)
        if b * PIECES % blocks == 0:
            for copy in copies[b * PIECES // blocks]:
                copy.wait()
        crow[b] = cum[b * PAD : (b + 1) * PAD, :]
        columns = columns_of(by_token, b)
        wide = wide_all(columns, heads)
        block_total = wide[BLOCK - 1 :, :]
        shrunk = value[rows, :].astype(F32) * jnp.exp2(block_total - wide)
        key_t = key[rows, :].T
        block_state = compact(mm(cat([key_t, key_t], 1), cat(split2(shrunk), 0)))
        state_blocks[b] = block_state
        state = jnp.exp2(block_total) * state + block_state
        total = total + block_total
    message[:HEAD_DIM, :] = state
    message[HEAD_DIM:, :] = jnp.broadcast_to(total, (PAD, lanes))


def inside_kernel(
    heads, blocks, query, key, value, crow, ccol, out, later, earlier, scores_high, scores_low
):
    def step(b, carry):
        rows = rows_of(b)
        crow_block = crow[b]
        columns = columns_of(ccol, b)
        q, k = query[rows, :], key[rows, :]
        scores, scores_t = [], []
        for p in range(heads // 2):
            side = lanes_of(p)
            across = slice(2 * p * BLOCK, 2 * (p + 1) * BLOCK)
            expos = exponents(columns, crow_block, p)
            weights, flipped = pair_weights(expos, False), pair_weights(expos, True)
            later[rows, across] = weights
            earlier[rows, across] = flipped
            scores.append(mm(q[:, side], apart(k[:, side].T)) * weights)
            scores_t.append(mm(k[:, side], apart(q[:, side].T)) * flipped)
        out[rows, :] = fold(mm(cat(split2(cat(scores, 1)), 0), spread_heads(value[rows, :])))
        high, low = split2(cat(scores_t, 1))
        scores_high[rows, :] = high
        scores_low[rows, :] = low
        return carry

    loop(blocks, step, 0)


def output_kernel(
    heads, blocks, mask, query, ccol, inside, before, other, state_blocks, out_t, states
):
    def step(b, state):
        rows = rows_of(b)
        states[b] = state
        columns = columns_of(ccol, b)
        wide = wide_all(columns, heads)
        q = query[rows, :]
        carried = mm(cat([q, q], 1), cat(wide_state(state), 0))
        block_out = (inside[rows, :] + jnp.exp2(wide) * carried).astype(BF16)
        out_t[:, rows] = block_out.T
        return jnp.exp2(wide[BLOCK - 1 :, :]) * state + state_blocks[b]

    first = entering(takes_from(mask, True), before, other)
    states[blocks] = loop(blocks, step, first)


def swap_of(direct):
    column = lax.axis_index("fsdp")
    return lax.axis_index("tm") ^ column if direct else column


def inner_kernel(heads, blocks, count, direct, swapped, refs):
    swap = swap_of(direct)
    weights = refs[:count]
    columns_in = refs[count : 2 * count]
    query, ccol, grad_high, grad_low, back_blocks, message, held, total = refs[2 * count :]
    lanes = heads * HEAD_DIM
    for k in range(count):
        if swapped and k >= 2:
            held[k ^ lax.axis_index("groups")] = weights[k][...]
        else:
            held[k] = weights[k][...]
    for j in range(count):
        part = mm(columns_in[j][...], held[swap ^ j], NT)
        total[...] = part if j == 0 else total[...] + part

    def step(i, carry):
        back, decayed = carry
        b = blocks - 1 - i
        rows = rows_of(b)
        columns = columns_of(ccol, b)
        wide = wide_all(columns, heads)
        block_total = wide[BLOCK - 1 :, :]
        grad = total[rows, :]
        high, low = split2(grad)
        grad_high[rows, :] = high
        grad_low[rows, :] = low
        query_t = query[rows, :].T
        grown = split2(grad * jnp.exp2(wide))
        block_back = compact(mm(cat([query_t, query_t], 1), cat(grown, 0)))
        back_blocks[b] = block_back
        return jnp.exp2(block_total) * back + block_back, decayed + block_total

    carry = (jnp.zeros((HEAD_DIM, lanes), F32), jnp.zeros((1, lanes), F32))
    back, decayed = loop(blocks, step, carry)
    message[:HEAD_DIM, :] = back
    message[HEAD_DIM:, :] = jnp.broadcast_to(decayed, (PAD, lanes))


def weight_kernel(count, direct, refs):
    swap = swap_of(direct)
    out_t = refs[0]
    columns = refs[1 : 1 + count]
    outs = refs[1 + count : 1 + 2 * count]
    held = refs[1 + 2 * count]
    for j in range(count):
        held[j] = mm(out_t[...], columns[j][...])
    for k in range(count):
        outs[k][...] = held[swap ^ k].astype(outs[k].dtype)


def head_columns(terms, b, blocks):
    lanes, width = terms.shape[1], blocks * PAD
    pick = ones_where(
        iota((lanes, width), 0) // HEAD_DIM + b * PAD == iota((lanes, width), 1)
    )
    return fold(mm(cat(split2(terms), 0), pick))


def query_kernel(
    heads, blocks, query, key, value, grad_high, grad_low, ccol, states, later,
    query_grad, query_terms,
):
    def step(b, carry):
        rows = rows_of(b)
        k, v = key[rows, :], value[rows, :]
        gh, gl = grad_high[rows, :], grad_low[rows, :]
        scores = []
        for p in range(heads // 2):
            side = lanes_of(p)
            v_apart = apart(v[:, side].T)
            both = cat([gh[:, side], gl[:, side]], 1)
            scores.append(mm(both, cat([v_apart, v_apart], 0)))
        weighed = split2(cat(scores, 1) * later[rows, :])
        state_high, state_low = wide_state(states[b])
        carried = fold(mm(cat([gh, gl], 0), turned(state_high))) + mm(gh, turned(state_low))
        full = jnp.exp2(wide_all(columns_of(ccol, b), heads)) * carried
        full = full + fold(mm(cat(weighed, 0), spread_heads(k)))
        query_grad[rows, :] = full.astype(BF16)
        return carry + head_columns(query[rows, :].astype(F32) * full, b, blocks)

    query_terms[...] = loop(blocks, step, jnp.zeros((BLOCK, blocks * PAD), F32))


def source_kernel(
    heads, blocks, query, value, grad_high, grad_low, earlier, scores_high, scores_low,
    key_inside, value_inside,
):
    def step(b, carry):
        rows = rows_of(b)
        v = value[rows, :]
        gh, gl = grad_high[rows, :], grad_low[rows, :]
        scores = []
        for p in range(heads // 2):
            side = lanes_of(p)
            both = cat([apart(gh[:, side].T), apart(gl[:, side].T)], 0)
            scores.append(mm(cat([v[:, side], v[:, side]], 1), both))
        weighed = split2(cat(scores, 1) * earlier[rows, :])
        high, low = scores_high[rows, :], scores_low[rows, :]
        value_inside[rows, :] = fold(mm(cat([high, low], 0), spread_heads(gh))) + mm(
            high, spread_heads(gl)
        )
        key_inside[rows, :] = fold(mm(cat(weighed, 0), spread_heads(query[rows, :])))
        return carry

    loop(blocks, step, 0)


def final_kernel(
    heads, blocks, mask, key, value, ccol, states, before, other, back_blocks, query_terms,
    key_inside, value_inside, *rest,
):
    parts, (key_grad, value_grad, decay_grad, weight_grad, tail_rows) = rest[:-5], rest[-5:]
    lanes = heads * HEAD_DIM
    weight_grad[...] = sum(part[...].astype(F32) for part in parts)

    def step(i, carry):
        back, terms = carry
        b = blocks - 1 - i
        rows = rows_of(b)
        columns = columns_of(ccol, b)
        k, v = key[rows, :], value[rows, :]
        wide = wide_all(columns, heads)
        block_total = wide[BLOCK - 1 :, :]
        shrink = jnp.exp2(block_total - wide)
        back_high, back_low = wide_state(back)
        carried = mm(cat([v, v], 1), cat([turned(back_high), turned(back_low)], 0))
        key_full = key_inside[rows, :] + shrink * carried
        carried = mm(cat([k, k], 1), cat([back_high, back_low], 0))
        value_full = value_inside[rows, :] + shrink * carried
        key_grad[rows, :] = key_full.astype(BF16)
        value_grad[rows, :] = value_full.astype(BF16)
        terms = terms - head_columns(k.astype(F32) * key_full, b, blocks)
        tail_rows[b] = jnp.broadcast_to(
            jnp.sum(states[b + 1] * back, axis=0, keepdims=True), (PAD, lanes)
        )
        return jnp.exp2(block_total) * back + back_blocks[b], terms

    first = entering(takes_from(mask, False), before, other)
    _, terms = loop(blocks, step, (first, query_terms[...]))
    lower = ones_where(iota((BLOCK, BLOCK), 0) >= iota((BLOCK, BLOCK), 1))
    sums = mm(cat(split3(terms.T), 0), lower)
    size = blocks * PAD
    sums = sums[:size, :] + sums[size : 2 * size, :] + sums[2 * size :, :]
    tails = cat([tail_rows[b] for b in range(blocks)], 0)
    pick = ones_where(iota((PAD, lanes), 1) // HEAD_DIM == iota((PAD, lanes), 0))
    ends = sum(mm(pick, part, NT) for part in split3(tails))
    for b in range(blocks):
        end = jnp.broadcast_to(ends[:, b * PAD : b * PAD + 1], (PAD, BLOCK))
        both = sums[b * PAD : (b + 1) * PAD, :] + end
        decay_grad[:, rows_of(b)] = both[:heads, :]


def combine_kernel(first, mask, ahead, mine, other, *refs):
    inside = None if first else refs[0]
    sent, kept = refs[-2:]
    takes = takes_from(mask, ahead)
    group, total = mine[:HEAD_DIM, :], mine[HEAD_DIM:, :]
    other_group, other_total = other[:HEAD_DIM, :], other[HEAD_DIM:, :]
    if first:
        state, decayed = jnp.zeros_like(group), jnp.zeros_like(total)
    else:
        state, decayed = inside[:HEAD_DIM, :], inside[HEAD_DIM:, :]
    kept[:HEAD_DIM, :] = jnp.where(takes, state + jnp.exp2(decayed[:1, :]) * other_group, state)
    kept[HEAD_DIM:, :] = jnp.where(takes, decayed + other_total, decayed)
    sent[:HEAD_DIM, :] = jnp.where(
        takes,
        jnp.exp2(total[:1, :]) * other_group + group,
        jnp.exp2(other_total[:1, :]) * group + other_group,
    )
    sent[HEAD_DIM:, :] = total + other_total


def shape(dims, dtype=F32):
    return jax.ShapeDtypeStruct(dims, dtype)


def call(kernel, outs, scratch=(), name=None, far=False):
    def run(*args):
        vmem = pl.BlockSpec(memory_space=pltpu.VMEM)
        return pl.pallas_call(
            kernel,
            out_shape=outs,
            in_specs=[pl.BlockSpec(memory_space=pltpu.HBM) if far else vmem] * len(args),
            out_specs=jax.tree.map(lambda _: vmem, outs),
            scratch_shapes=list(scratch),
            compiler_params=pltpu.CompilerParams(vmem_limit_bytes=GRANT),
            cost_estimate=pl.CostEstimate(
                flops=COST.get(name, 1) * 1_000_000_000, bytes_accessed=0, transcendentals=0
            ),
        )(*args)

    return run


def swap_with(value, axis, size, mask):
    return lax.ppermute(value, axis, [(i, i ^ mask) for i in range(size)])


def passed_states(message, axis, size, ahead, name):
    inside = jnp.zeros_like(message)
    mask = 1
    while True:
        other = swap_with(message, axis, size, mask)
        if mask * 2 >= size:
            return mask, inside, other
        first = mask == 1
        message, inside = call(
            functools.partial(combine_kernel, first, mask, ahead),
            (shape(message.shape), shape(message.shape)),
            name=name,
        )(message, other, *([] if first else [inside]))
        mask *= 2


def crossed(groups, tm):
    return groups == 2 and tm == 4


def gathered_shares(share, groups, tm):
    out = [share]
    for k in range(1, 2 if crossed(groups, tm) else tm):
        out.append(swap_with(share, "tm", tm, k))
    if crossed(groups, tm):
        pairs = [(g * tm + i, g * tm + (i ^ (2 + g))) for g in range(groups) for i in range(tm)]
        out.append(lax.ppermute(share, ("groups", "tm"), pairs))
        out.append(swap_with(out[-1], "groups", groups, 1))
    return out


def local(sizes, query, key, value, decay, out_grad, out_weight):
    groups, tm, fsdp = sizes
    rows, lanes = query.shape
    heads = lanes // HEAD_DIM
    blocks = rows // BLOCK
    direct = tm == fsdp and tm & (tm - 1) == 0

    order = {0: out_grad}
    mask = fsdp // 2
    while mask:
        for held in list(order):
            order[held | mask] = swap_with(order[held], "fsdp", fsdp, mask)
        mask //= 2
    columns = [order[j] for j in range(fsdp)]

    if direct:
        weights = gathered_shares(out_weight, groups, tm)
    else:
        whole = lax.all_gather(out_weight, "tm", axis=1, tiled=True)
        weights = jnp.split(whole, fsdp, axis=1)

    crow_shape = shape((blocks, PAD, BLOCK))
    message_shape = shape((HEAD_DIM + PAD, lanes))
    crow, ccol, state_blocks, message = call(
        functools.partial(summary_kernel, heads, blocks),
        (
            crow_shape,
            shape((BLOCK, blocks * PAD)),
            shape((blocks, HEAD_DIM, lanes)),
            message_shape,
        ),
        scratch=[
            pltpu.VMEM((heads, rows), F32),
            pltpu.VMEM((rows, lanes), BF16),
            pltpu.VMEM((rows, lanes), BF16),
            pltpu.SemaphoreType.DMA(()),
            pltpu.SemaphoreType.DMA((2, PIECES)),
        ],
        name="summary",
        far=True,
    )(*(pltpu.with_memory_space_constraint(x, pltpu.HBM) for x in (decay.T, key, value)))
    mask, before, other = passed_states(message, "tm", tm, True, "combine_ahead")
    pairs = heads * BLOCK
    inside, later, earlier, scores_high, scores_low = call(
        functools.partial(inside_kernel, heads, blocks),
        (
            shape((rows, lanes)),
            shape((rows, pairs)),
            shape((rows, pairs)),
            shape((rows, pairs), BF16),
            shape((rows, pairs), BF16),
        ),
        name="inside",
    )(query, key, value, crow, ccol)
    out_t, states = call(
        functools.partial(output_kernel, heads, blocks, mask),
        (shape((lanes, rows), BF16), shape((blocks + 1, HEAD_DIM, lanes))),
        name="outputs",
    )(query, ccol, inside, before, other, state_blocks)

    width = out_grad.shape[1]
    sent = BF16 if direct else F32
    partials = call(
        lambda *refs: weight_kernel(fsdp, direct, refs),
        tuple(shape((lanes, width), F32 if k == 0 else sent) for k in range(fsdp)),
        scratch=[pltpu.VMEM((fsdp, lanes, width), F32)],
        name="weight",
    )(out_t, *columns)
    if direct:
        received = []
        for k in range(1, tm):
            received.append(swap_with(partials[k], "tm", tm, k))
    else:
        partials = [
            lax.psum_scatter(
                jnp.concatenate(partials, axis=1), "tm", scatter_dimension=1, tiled=True
            )
        ]
        received = []

    grad_high, grad_low, back_blocks, message = call(
        lambda *refs: inner_kernel(heads, blocks, fsdp, direct, direct and crossed(groups, tm), refs),
        (
            shape((rows, lanes), BF16),
            shape((rows, lanes), BF16),
            shape((blocks, HEAD_DIM, lanes)),
            message_shape,
        ),
        scratch=[pltpu.VMEM((fsdp, lanes, width), BF16), pltpu.VMEM((rows, lanes), F32)],
        name="inner",
    )(*weights, *columns, query, ccol)
    mask, before, other = passed_states(message, "tm", tm, False, "combine_back")

    query_grad, query_terms = call(
        functools.partial(query_kernel, heads, blocks),
        (shape((rows, lanes), BF16), shape((BLOCK, blocks * PAD))),
        name="queries",
    )(query, key, value, grad_high, grad_low, ccol, states, later)
    key_inside, value_inside = call(
        functools.partial(source_kernel, heads, blocks),
        (shape((rows, lanes)), shape((rows, lanes))),
        name="sources",
    )(query, value, grad_high, grad_low, earlier, scores_high, scores_low)
    key_grad, value_grad, decay_grad, weight_grad = call(
        functools.partial(final_kernel, heads, blocks, mask),
        (
            shape((rows, lanes), BF16),
            shape((rows, lanes), BF16),
            shape((heads, rows)),
            shape(partials[0].shape),
        ),
        scratch=[pltpu.VMEM((blocks, PAD, lanes), F32)],
        name="final",
    )(
        key, value, ccol, states, before, other, back_blocks, query_terms, key_inside,
        value_inside, partials[0], *received,
    )
    return query_grad, key_grad, value_grad, decay_grad.T, weight_grad


def solution(mesh):
    wide = P(("groups", "tm"), "fsdp")
    sizes = (mesh.shape["groups"], mesh.shape["tm"], mesh.shape["fsdp"])

    def body(*args):
        return local(sizes, *args)

    return jax.shard_map(
        body,
        mesh=mesh,
        in_specs=(wide, wide, wide, wide, wide, P("fsdp", "tm")),
        out_specs=(wide, wide, wide, wide, P(("groups", "fsdp"), "tm")),
        check_vma=False,
    )
```

profile of v0, /device:TPU:0, one launch (start us, length us, event | category | flops | bytes accessed | tf_op | source)
XLA Modules:
  0.0 48.3 jit_solution(11623557379294409395)
XLA Ops:
  0.6 3.0 %collective-permute-start.4 = (bf16[1024,256]{1,0:T(8,128)(2,1)}, bf16[1024,256]{1,0:T(8,128)(2,1)S(1)}, u32[]{:S(2)}, u32[]{:S(2)}) collective-permute-start(bf16[1024,256]{1,0:T(8,128)(2,1)} %refs_1_.1), channel_id=1, source_target_pairs={{0,2},{1,3},{2,0},{3,1},{4,6},{5,7},{6,4},{7,5},{8,10},{9,11},{10,... | collective-permute-start | bytes 1572872 | tf_op jit(solution)/shard_map/ppermute | solution.py:459
  3.7 2.7 %shard_map.101 = (f32[8,8,128]{2,1,0:T(8,128)S(1)}, f32[128,64]{1,0:T(8,128)S(1)}, f32[8,64,256]{2,1,0:T(8,128)S(1)}, f32[72,256]{1,0:T(8,128)S(1)}) custom-call(f32[4,1024]{1,0:T(4,128)} %bitcast.2, bf16[1024,256]{1,0:T(8,128)(2,1)} %key.5, bf16[1024,256]{1,0:T(8,128)(2,1)} %value.7), custom_call_target="tpu_custom_call" | custom-call | flops 3000000000 | tf_op jit(solution)/shard_map/pallas_call | solution.py:443
  6.4 1.6 %collective-permute-start.6 = (f32[72,256]{1,0:T(8,128)S(1)}, f32[72,256]{1,0:T(8,128)S(1)}, u32[]{:S(2)}, u32[]{:S(2)}) collective-permute-start(f32[72,256]{1,0:T(8,128)S(1)} %get-tuple-element.41.mine), channel_id=1, source_target_pairs={{0,4},{4,0},{8,12},{12,8},{1,5},{5,1},{9,13},{13,9},{2,6},{6,2},{1... | collective-permute-start | bytes 221192 | tf_op jit(solution)/shard_map/ppermute | solution.py:459
  8.0 0.4 collective-permute-start
  8.5 2.6 %collective-permute-start.1 = (bf16[256,256]{1,0:T(8,128)(2,1)S(1)}, bf16[256,256]{1,0:T(8,128)(2,1)S(1)}, u32[]{:S(2)}, u32[]{:S(2)}) collective-permute-start(bf16[256,256]{1,0:T(8,128)(2,1)S(1)} %copy-done.4), channel_id=1, source_target_pairs={{0,8},{4,12},{8,0},{12,4},{16,28},{20,24},{24,20},{28,16},{1,9},{5... | collective-permute-start | bytes 393224 | tf_op jit(solution)/shard_map/ppermute | solution.py:488
  11.1 1.9 %collective-permute-done.6.other = f32[72,256]{1,0:T(8,128)S(1)} collective-permute-done((f32[72,256]{1,0:T(8,128)S(1)}, f32[72,256]{1,0:T(8,128)S(1)}, u32[]{:S(2)}, u32[]{:S(2)}) %collective-permute-start.6) | collective-permute-done | bytes 73760 | tf_op jit(solution)/shard_map/ppermute | solution.py:459
  13.0 1.2 %collective-permute-start.7 = (f32[72,256]{1,0:T(8,128)S(1)}, f32[72,256]{1,0:T(8,128)S(1)}, u32[]{:S(2)}, u32[]{:S(2)}) collective-permute-start(f32[72,256]{1,0:T(8,128)S(1)} %get-tuple-element.43), channel_id=1, source_target_pairs={{0,8},{4,12},{8,0},{12,4},{1,9},{5,13},{9,1},{13,5},{2,10},{6,14},... | collective-permute-start | bytes 221192 | tf_op jit(solution)/shard_map/ppermute | solution.py:459
  14.3 1.5 %collective-permute-done.4.refs_6_.refs_3_ = bf16[1024,256]{1,0:T(8,128)(2,1)S(1)} collective-permute-done((bf16[1024,256]{1,0:T(8,128)(2,1)}, bf16[1024,256]{1,0:T(8,128)(2,1)S(1)}, u32[]{:S(2)}, u32[]{:S(2)}) %collective-permute-start.4) | collective-permute-done | bytes 524320 | tf_op jit(solution)/shard_map/ppermute | solution.py:459
  15.8 1.8 %shard_map.103 = (f32[1024,256]{1,0:T(8,128)S(1)}, f32[1024,512]{1,0:T(8,128)S(1)}, f32[1024,512]{1,0:T(8,128)S(1)}, bf16[1024,512]{1,0:T(8,128)(2,1)S(1)}, bf16[1024,512]{1,0:T(8,128)(2,1)S(1)}) custom-call(bf16[1024,256]{1,0:T(8,128)(2,1)S(1)} %copy-done.1, bf16[1024,256]{1,0:T(8,128)(2,1)S(1)} %copy-done.2, bf16[1024,256]{1,0:T(8,128)(2,1)S(1)} %copy-done.3, ...), custom_call_target="tpu_custom_call" | custom-call | flops 4000000000 | tf_op jit(solution)/shard_map/pallas_call | solution.py:443
  17.7 3.1 %collective-permute-start.2 = (bf16[256,256]{1,0:T(8,128)(2,1)S(1)}, bf16[256,256]{1,0:T(8,128)(2,1)S(1)}, u32[]{:S(2)}, u32[]{:S(2)}) collective-permute-start(bf16[256,256]{1,0:T(8,128)(2,1)S(1)} %collective-permute-done.1.refs_2_), channel_id=1, source_target_pairs={{0,16},{16,0},{1,17},{17,1},{2,18},{18,2},{3,19},{19,3},{4,20},{20... | collective-permute-start | bytes 393224 | tf_op jit(solution)/shard_map/ppermute | solution.py:459
  20.8 1.5 %shard_map.105 = (bf16[256,1024]{1,0:T(8,128)(2,1)S(1)}, f32[9,64,256]{2,1,0:T(8,128)S(1)}) custom-call(bf16[1024,256]{1,0:T(8,128)(2,1)S(1)} %copy-done.1, f32[128,64]{1,0:T(8,128)S(1)} %get-tuple-element.36.refs_9_.ccol, f32[1024,256]{1,0:T(8,128)S(1)} %get-tuple-element.40.inside, f32[72,256]{1,0:T(8,128)S(1)} %get-tuple-element.42.before, ...), custom_call_target="tpu_custom_call" | custom-call | flops 3000000000 | tf_op jit(solution)/shard_map/pallas_call | solution.py:443
  22.3 1.3 %collective-permute-done.2.refs_3_ = bf16[256,256]{1,0:T(8,128)(2,1)S(1)} collective-permute-done((bf16[256,256]{1,0:T(8,128)(2,1)S(1)}, bf16[256,256]{1,0:T(8,128)(2,1)S(1)}, u32[]{:S(2)}, u32[]{:S(2)}) %collective-permute-start.2) | collective-permute-done | bytes 131104 | tf_op jit(solution)/shard_map/ppermute | solution.py:459
  23.7 1.7 %shard_map.102 = (bf16[1024,256]{1,0:T(8,128)(2,1)S(1)}, bf16[1024,256]{1,0:T(8,128)(2,1)S(1)}, f32[8,64,256]{2,1,0:T(8,128)S(1)}, f32[72,256]{1,0:T(8,128)S(1)}) custom-call(bf16[256,256]{1,0:T(8,128)(2,1)S(1)} %copy-done.4, bf16[256,256]{1,0:T(8,128)(2,1)S(1)} %collective-permute-done.refs_1_, bf16[256,256]{1,0:T(8,128)(2,1)S(1)} %collective-permute-done.1.refs_2_, ...), custom_call_target="tpu_custom_call" | custom-call | flops 3000000000 | tf_op jit(solution)/shard_map/pallas_call | solution.py:443
  25.4 1.8 %collective-permute-start.8 = (f32[72,256]{1,0:T(8,128)S(1)}, f32[72,256]{1,0:T(8,128)S(1)}, u32[]{:S(2)}, u32[]{:S(2)}) collective-permute-start(f32[72,256]{1,0:T(8,128)S(1)} %get-tuple-element.48.mine), channel_id=1, source_target_pairs={{0,4},{4,0},{8,12},{12,8},{1,5},{5,1},{9,13},{13,9},{2,6},{6,2},{1... | collective-permute-start | bytes 221192 | tf_op jit(solution)/shard_map/ppermute | solution.py:459
  27.3 0.8 %shard_map.109 = (f32[256,256]{1,0:T(8,128)S(1)}, bf16[256,256]{1,0:T(8,128)(2,1)S(1)}, bf16[256,256]{1,0:T(8,128)(2,1)S(1)}, bf16[256,256]{1,0:T(8,128)(2,1)S(1)}) custom-call(bf16[256,1024]{1,0:T(8,128)(2,1)S(1)} %get-tuple-element.58.refs_0_, bf16[1024,256]{1,0:T(8,128)(2,1)S(1)} %copy-done, bf16[1024,256]{1,0:T(8,128)(2,1)S(1)} %collective-permute-done.3.refs_5_.refs_2_, ...), custom_call_target="tpu_custom_call" | custom-call | flops 2000000000 | tf_op jit(solution)/shard_map/pallas_call | solution.py:443
  28.0 0.3 collective-permute-start.10
  28.3 2.8 %collective-permute-start.11 = (bf16[256,256]{1,0:T(8,128)(2,1)S(1)}, bf16[256,256]{1,0:T(8,128)(2,1)S(1)}, u32[]{:S(2)}, u32[]{:S(2)}) collective-permute-start(bf16[256,256]{1,0:T(8,128)(2,1)S(1)} %get-tuple-element.61), channel_id=1, source_target_pairs={{0,8},{4,12},{8,0},{12,4},{1,9},{5,13},{9,1},{13,5},{2,10},{6,14},... | collective-permute-start | bytes 393224 | tf_op jit(solution)/shard_map/ppermute | solution.py:459
  31.1 1.3 %collective-permute-start.12 = (bf16[256,256]{1,0:T(8,128)(2,1)S(1)}, bf16[256,256]{1,0:T(8,128)(2,1)S(1)}, u32[]{:S(2)}, u32[]{:S(2)}) collective-permute-start(bf16[256,256]{1,0:T(8,128)(2,1)S(1)} %get-tuple-element.62), channel_id=1, source_target_pairs={{0,12},{4,8},{8,4},{12,0},{1,13},{5,9},{9,5},{13,1},{2,14},{6,10},... | collective-permute-start | bytes 393224 | tf_op jit(solution)/shard_map/ppermute | solution.py:459
  32.5 3.8 %shard_map.106 = (bf16[1024,256]{1,0:T(8,128)(2,1)}, f32[128,64]{1,0:T(8,128)S(1)}) custom-call(bf16[1024,256]{1,0:T(8,128)(2,1)S(1)} %copy-done.1, bf16[1024,256]{1,0:T(8,128)(2,1)S(1)} %copy-done.2, bf16[1024,256]{1,0:T(8,128)(2,1)S(1)} %copy-done.3, bf16[1024,256]{1,0:T(8,128)(2,1)S(1)} %get-tuple-element.37.grad_high, ...), custom_call_target="tpu_custom_call" | custom-call | flops 4000000000 | tf_op jit(solution)/shard_map/pallas_call | solution.py:443
  36.3 1.8 %collective-permute-start.9 = (f32[72,256]{1,0:T(8,128)S(1)}, f32[72,256]{1,0:T(8,128)S(1)}, u32[]{:S(2)}, u32[]{:S(2)}) collective-permute-start(f32[72,256]{1,0:T(8,128)S(1)} %get-tuple-element.50), channel_id=1, source_target_pairs={{0,8},{4,12},{8,0},{12,4},{1,9},{5,13},{9,1},{13,5},{2,10},{6,14},... | collective-permute-start | bytes 221192 | tf_op jit(solution)/shard_map/ppermute | solution.py:459
  38.1 1.9 %shard_map.108 = (f32[1024,256]{1,0:T(8,128)S(1)}, f32[1024,256]{1,0:T(8,128)S(1)}) custom-call(bf16[1024,256]{1,0:T(8,128)(2,1)S(1)} %copy-done.1, bf16[1024,256]{1,0:T(8,128)(2,1)S(1)} %copy-done.3, bf16[1024,256]{1,0:T(8,128)(2,1)S(1)} %get-tuple-element.37.grad_high, bf16[1024,256]{1,0:T(8,128)(2,1)S(1)} %get-tuple-element.38.grad_low, ...), custom_call_target="tpu_custom_call" | custom-call | flops 4000000000 | tf_op jit(solution)/shard_map/pallas_call | solution.py:443
  40.0 2.8 %collective-permute-done.11.rest_2_ = bf16[256,256]{1,0:T(8,128)(2,1)S(1)} collective-permute-done((bf16[256,256]{1,0:T(8,128)(2,1)S(1)}, bf16[256,256]{1,0:T(8,128)(2,1)S(1)}, u32[]{:S(2)}, u32[]{:S(2)}) %collective-permute-start.11) | collective-permute-done | bytes 131104 | tf_op jit(solution)/shard_map/ppermute | solution.py:459
  42.8 2.8 %collective-permute-done.9.other = f32[72,256]{1,0:T(8,128)S(1)} collective-permute-done((f32[72,256]{1,0:T(8,128)S(1)}, f32[72,256]{1,0:T(8,128)S(1)}, u32[]{:S(2)}, u32[]{:S(2)}) %collective-permute-start.9) | collective-permute-done | bytes 73760 | tf_op jit(solution)/shard_map/ppermute | solution.py:459
  45.6 2.7 %shard_map.110 = (bf16[1024,256]{1,0:T(8,128)(2,1)}, bf16[1024,256]{1,0:T(8,128)(2,1)}, f32[4,1024]{1,0:T(4,128)}, f32[256,256]{1,0:T(8,128)}) custom-call(bf16[1024,256]{1,0:T(8,128)(2,1)S(1)} %copy-done.2, bf16[1024,256]{1,0:T(8,128)(2,1)S(1)} %copy-done.3, f32[128,64]{1,0:T(8,128)S(1)} %get-tuple-element.36.refs_9_.ccol, ...), custom_call_target="tpu_custom_call" | custom-call | flops 4000000000 | tf_op jit(solution)/shard_map/pallas_call | solution.py:443
  (22 shorter events, 0.2 us)
Async XLA Ops:
  0.6 15.2 %collective-permute-start.4 = (bf16[1024,256]{1,0:T(8,128)(2,1)}, bf16[1024,256]{1,0:T(8,128)(2,1)S(1)}, u32[]{:S(2)}, u32[]{:S(2)}) collective-permute-start(bf16[1024,256]{1,0:T(8,128)(2,1)} %refs_1_.1), channel_id=1, source_target_pairs={{0,2},{1,3},{2,0},{3,1},{4,6},{5,7},{6,4},{7,5},{8,10},{9,11},{10,... | collective-permute-start | bytes 1572872 | tf_op jit(solution)/shard_map/ppermute | solution.py:459
  3.7 4.3 %copy-start.4 = (bf16[256,256]{1,0:T(8,128)(2,1)S(1)}, bf16[256,256]{1,0:T(8,128)(2,1)}, u32[]{:S(2)}) copy-start(bf16[256,256]{1,0:T(8,128)(2,1)} %refs_0_.1) | copy-start | bytes 393220
  3.7 7.4 %copy-start = (bf16[1024,256]{1,0:T(8,128)(2,1)S(1)}, bf16[1024,256]{1,0:T(8,128)(2,1)}, u32[]{:S(2)}) copy-start(bf16[1024,256]{1,0:T(8,128)(2,1)} %refs_1_.1) | copy-start | bytes 1572868
  6.3 9.5 %copy-start.1 = (bf16[1024,256]{1,0:T(8,128)(2,1)S(1)}, bf16[1024,256]{1,0:T(8,128)(2,1)}, u32[]{:S(2)}) copy-start(bf16[1024,256]{1,0:T(8,128)(2,1)} %query.7) | copy-start | bytes 1572868
  6.3 9.5 %copy-start.2 = (bf16[1024,256]{1,0:T(8,128)(2,1)S(1)}, bf16[1024,256]{1,0:T(8,128)(2,1)}, u32[]{:S(2)}) copy-start(bf16[1024,256]{1,0:T(8,128)(2,1)} %key.5) | copy-start | bytes 1572868
  6.4 9.5 %copy-start.3 = (bf16[1024,256]{1,0:T(8,128)(2,1)S(1)}, bf16[1024,256]{1,0:T(8,128)(2,1)}, u32[]{:S(2)}) copy-start(bf16[1024,256]{1,0:T(8,128)(2,1)} %value.7) | copy-start | bytes 1572868
  6.4 6.6 %collective-permute-start.6 = (f32[72,256]{1,0:T(8,128)S(1)}, f32[72,256]{1,0:T(8,128)S(1)}, u32[]{:S(2)}, u32[]{:S(2)}) collective-permute-start(f32[72,256]{1,0:T(8,128)S(1)} %get-tuple-element.41.mine), channel_id=1, source_target_pairs={{0,4},{4,0},{8,12},{12,8},{1,5},{5,1},{9,13},{13,9},{2,6},{6,2},{1... | collective-permute-start | bytes 221192 | tf_op jit(solution)/shard_map/ppermute | solution.py:459
  8.0 14.3 %collective-permute-start = (bf16[256,256]{1,0:T(8,128)(2,1)S(1)}, bf16[256,256]{1,0:T(8,128)(2,1)S(1)}, u32[]{:S(2)}, u32[]{:S(2)}) collective-permute-start(bf16[256,256]{1,0:T(8,128)(2,1)S(1)} %copy-done.4), channel_id=1, source_target_pairs={{0,4},{4,0},{8,12},{12,8},{1,5},{5,1},{9,13},{13,9},{2,6},{6,2},{1... | collective-permute-start | bytes 393224 | tf_op jit(solution)/shard_map/ppermute | solution.py:459
  8.5 9.2 %collective-permute-start.1 = (bf16[256,256]{1,0:T(8,128)(2,1)S(1)}, bf16[256,256]{1,0:T(8,128)(2,1)S(1)}, u32[]{:S(2)}, u32[]{:S(2)}) collective-permute-start(bf16[256,256]{1,0:T(8,128)(2,1)S(1)} %copy-done.4), channel_id=1, source_target_pairs={{0,8},{4,12},{8,0},{12,4},{16,28},{20,24},{24,20},{28,16},{1,9},{5... | collective-permute-start | bytes 393224 | tf_op jit(solution)/shard_map/ppermute | solution.py:488
  11.1 12.6 %collective-permute-start.3 = (bf16[1024,256]{1,0:T(8,128)(2,1)S(1)}, bf16[1024,256]{1,0:T(8,128)(2,1)S(1)}, u32[]{:S(2)}, u32[]{:S(2)}) collective-permute-start(bf16[1024,256]{1,0:T(8,128)(2,1)S(1)} %copy-done), channel_id=1, source_target_pairs={{0,1},{1,0},{2,3},{3,2},{4,5},{5,4},{6,7},{7,6},{8,9},{9,8},{10,11... | collective-permute-start | bytes 1572872 | tf_op jit(solution)/shard_map/ppermute | solution.py:459
  13.0 7.8 %collective-permute-start.7 = (f32[72,256]{1,0:T(8,128)S(1)}, f32[72,256]{1,0:T(8,128)S(1)}, u32[]{:S(2)}, u32[]{:S(2)}) collective-permute-start(f32[72,256]{1,0:T(8,128)S(1)} %get-tuple-element.43), channel_id=1, source_target_pairs={{0,8},{4,12},{8,0},{12,4},{1,9},{5,13},{9,1},{13,5},{2,10},{6,14},... | collective-permute-start | bytes 221192 | tf_op jit(solution)/shard_map/ppermute | solution.py:459
  15.8 7.9 %collective-permute-start.5 = (bf16[1024,256]{1,0:T(8,128)(2,1)S(1)}, bf16[1024,256]{1,0:T(8,128)(2,1)S(1)}, u32[]{:S(2)}, u32[]{:S(2)}) collective-permute-start(bf16[1024,256]{1,0:T(8,128)(2,1)S(1)} %collective-permute-done.4.refs_6_.refs_3_), channel_id=1, source_target_pairs={{0,1},{1,0},{2,3},{3,2},{4,5},{5,4},{6,7},{7,6},{8,9},{9,8},{10,11... | collective-permute-start | bytes 1572872 | tf_op jit(solution)/shard_map/ppermute | solution.py:459
  17.7 6.0 %collective-permute-start.2 = (bf16[256,256]{1,0:T(8,128)(2,1)S(1)}, bf16[256,256]{1,0:T(8,128)(2,1)S(1)}, u32[]{:S(2)}, u32[]{:S(2)}) collective-permute-start(bf16[256,256]{1,0:T(8,128)(2,1)S(1)} %collective-permute-done.1.refs_2_), channel_id=1, source_target_pairs={{0,16},{16,0},{1,17},{17,1},{2,18},{18,2},{3,19},{19,3},{4,20},{20... | collective-permute-start | bytes 393224 | tf_op jit(solution)/shard_map/ppermute | solution.py:459
  25.4 10.8 %collective-permute-start.8 = (f32[72,256]{1,0:T(8,128)S(1)}, f32[72,256]{1,0:T(8,128)S(1)}, u32[]{:S(2)}, u32[]{:S(2)}) collective-permute-start(f32[72,256]{1,0:T(8,128)S(1)} %get-tuple-element.48.mine), channel_id=1, source_target_pairs={{0,4},{4,0},{8,12},{12,8},{1,5},{5,1},{9,13},{13,9},{2,6},{6,2},{1... | collective-permute-start | bytes 221192 | tf_op jit(solution)/shard_map/ppermute | solution.py:459
  28.0 11.9 %collective-permute-start.10 = (bf16[256,256]{1,0:T(8,128)(2,1)S(1)}, bf16[256,256]{1,0:T(8,128)(2,1)S(1)}, u32[]{:S(2)}, u32[]{:S(2)}) collective-permute-start(bf16[256,256]{1,0:T(8,128)(2,1)S(1)} %get-tuple-element.60), channel_id=1, source_target_pairs={{0,4},{4,0},{8,12},{12,8},{1,5},{5,1},{9,13},{13,9},{2,6},{6,2},{1... | collective-permute-start | bytes 393224 | tf_op jit(solution)/shard_map/ppermute | solution.py:459
  28.3 14.5 %collective-permute-start.11 = (bf16[256,256]{1,0:T(8,128)(2,1)S(1)}, bf16[256,256]{1,0:T(8,128)(2,1)S(1)}, u32[]{:S(2)}, u32[]{:S(2)}) collective-permute-start(bf16[256,256]{1,0:T(8,128)(2,1)S(1)} %get-tuple-element.61), channel_id=1, source_target_pairs={{0,8},{4,12},{8,0},{12,4},{1,9},{5,13},{9,1},{13,5},{2,10},{6,14},... | collective-permute-start | bytes 393224 | tf_op jit(solution)/shard_map/ppermute | solution.py:459
  31.1 11.7 %collective-permute-start.12 = (bf16[256,256]{1,0:T(8,128)(2,1)S(1)}, bf16[256,256]{1,0:T(8,128)(2,1)S(1)}, u32[]{:S(2)}, u32[]{:S(2)}) collective-permute-start(bf16[256,256]{1,0:T(8,128)(2,1)S(1)} %get-tuple-element.62), channel_id=1, source_target_pairs={{0,12},{4,8},{8,4},{12,0},{1,13},{5,9},{9,5},{13,1},{2,14},{6,10},... | collective-permute-start | bytes 393224 | tf_op jit(solution)/shard_map/ppermute | solution.py:459
  36.3 9.3 %collective-permute-start.9 = (f32[72,256]{1,0:T(8,128)S(1)}, f32[72,256]{1,0:T(8,128)S(1)}, u32[]{:S(2)}, u32[]{:S(2)}) collective-permute-start(f32[72,256]{1,0:T(8,128)S(1)} %get-tuple-element.50), channel_id=1, source_target_pairs={{0,8},{4,12},{8,0},{12,4},{1,9},{5,13},{9,1},{13,5},{2,10},{6,14},... | collective-permute-start | bytes 221192 | tf_op jit(solution)/shard_map/ppermute | solution.py:459
where the time goes:
time: 48.5 us; the launch traced here: 48.3 us
  starting transfers between devices  20.1 us (41%)
  Pallas kernels  16.9 us (35%)
  waiting for transfers between devices  10.5 us (22%)
  between operations  0.76 us (2%)
    ppermute x12, starting transfers between devices, swap_with(): return lax.ppermute(value, axis, [(i, i ^ mask) for i in range(size)])  17.5 us
    pallas_call x10, Pallas kernels, run(): pl.pallas_call(kernel, out_shape=outs, in_specs=[pl.BlockSpec(memory_spac...  16.9 us
    ppermute x12, waiting for transfers between devices, swap_with(): return lax.ppermute(value, axis, [(i, i ^ mask) for i in range(size)])  10.5 us
    ppermute x1, starting transfers between devices, gathered_shares(): out.append(lax.ppermute(share, ('groups', 'tm'), pairs))  2.59 us
  transfers between devices with their start and end apart: 13, of which 6 were waited for; matrix products, arithmetic and copies ran while one was open for 0% of the time, Pallas kernels for 26%

commit v1 on v0

--- a/solution.py
+++ b/solution.py
@@ -345,11 +345,15 @@
 
 
 def source_kernel(
-    heads, blocks, query, value, grad_high, grad_low, earlier, scores_high, scores_low,
-    key_inside, value_inside,
+    heads, blocks, query, value, grad_high, grad_low, ccol, earlier, scores_high, scores_low,
+    key_inside, value_inside, shrinks, leaving,
 ):
     def step(b, carry):
         rows = rows_of(b)
+        wide = wide_all(columns_of(ccol, b), heads)
+        block_total = wide[BLOCK - 1 :, :]
+        shrinks[rows, :] = jnp.exp2(block_total - wide)
+        leaving[b] = jnp.broadcast_to(jnp.exp2(block_total), (PAD, wide.shape[1]))
         v = value[rows, :]
         gh, gl = grad_high[rows, :], grad_low[rows, :]
         scores = []
@@ -369,7 +373,7 @@
 
 
 def final_kernel(
-    heads, blocks, mask, key, value, ccol, states, before, other, back_blocks, query_terms,
+    heads, blocks, mask, key, value, shrinks, leaving, states, before, other, back_blocks, query_terms,
     key_inside, value_inside, *rest,
 ):
     parts, (key_grad, value_grad, decay_grad, weight_grad, tail_rows) = rest[:-5], rest[-5:]
@@ -380,11 +384,8 @@
         back, terms = carry
         b = blocks - 1 - i
         rows = rows_of(b)
-        columns = columns_of(ccol, b)
         k, v = key[rows, :], value[rows, :]
-        wide = wide_all(columns, heads)
-        block_total = wide[BLOCK - 1 :, :]
-        shrink = jnp.exp2(block_total - wide)
+        shrink = shrinks[rows, :]
         back_high, back_low = wide_state(back)
         carried = mm(cat([v, v], 1), cat([turned(back_high), turned(back_low)], 0))
         key_full = key_inside[rows, :] + shrink * carried
@@ -396,7 +397,7 @@
         tail_rows[b] = jnp.broadcast_to(
             jnp.sum(states[b + 1] * back, axis=0, keepdims=True), (PAD, lanes)
         )
-        return jnp.exp2(block_total) * back + back_blocks[b], terms
+        return leaving[b][:1, :] * back + back_blocks[b], terms
 
     first = entering(takes_from(mask, False), before, other)
     _, terms = loop(blocks, step, (first, query_terms[...]))
@@ -588,11 +589,16 @@
         (shape((rows, lanes), BF16), shape((BLOCK, blocks * PAD))),
         name="queries",
     )(query, key, value, grad_high, grad_low, ccol, states, later)
-    key_inside, value_inside = call(
+    key_inside, value_inside, shrinks, leaving = call(
         functools.partial(source_kernel, heads, blocks),
-        (shape((rows, lanes)), shape((rows, lanes))),
+        (
+            shape((rows, lanes)),
+            shape((rows, lanes)),
+            shape((rows, lanes)),
+            shape((blocks, PAD, lanes)),
+        ),
         name="sources",
-    )(query, value, grad_high, grad_low, earlier, scores_high, scores_low)
+    )(query, value, grad_high, grad_low, ccol, earlier, scores_high, scores_low)
     key_grad, value_grad, decay_grad, weight_grad = call(
         functools.partial(final_kernel, heads, blocks, mask),
         (
@@ -604,7 +610,7 @@
         scratch=[pltpu.VMEM((blocks, PAD, lanes), F32)],
         name="final",
     )(
-        key, value, ccol, states, before, other, back_blocks, query_terms, key_inside,
+        key, value, shrinks, leaving, states, before, other, back_blocks, query_terms, key_inside,
         value_inside, partials[0], *received,
     )
     return query_grad, key_grad, value_grad, decay_grad.T, weight_grad

time: 48.5 us -> 48.1 us (level)
  no operation moved by 1% of the time
where the time goes in v1:
time: 48.1 us; the launch traced here: 48 us
  starting transfers between devices  20.1 us (42%)
  Pallas kernels  16.6 us (35%)
  waiting for transfers between devices  10.5 us (22%)
  between operations  0.76 us (2%)
    ppermute x12, starting transfers between devices, swap_with(): return lax.ppermute(value, axis, [(i, i ^ mask) for i in range(size)])  17.5 us
    pallas_call x10, Pallas kernels, run(): pl.pallas_call(kernel, out_shape=outs, in_specs=[pl.BlockSpec(memory_spac...  16.6 us
    ppermute x12, waiting for transfers between devices, swap_with(): return lax.ppermute(value, axis, [(i, i ^ mask) for i in range(size)])  10.5 us
    ppermute x1, starting transfers between devices, gathered_shares(): out.append(lax.ppermute(share, ('groups', 'tm'), pairs))  2.59 us
  transfers between devices with their start and end apart: 13, of which 6 were waited for; matrix products, arithmetic and copies ran while one was open for 0% of the time, Pallas kernels for 26%

profile of v1, /device:TPU:0, one launch (start us, length us, event | category | flops | bytes accessed | tf_op | source)
XLA Modules:
  0.0 48.0 jit_solution(13341555993441851404)
XLA Ops:
  0.6 3.0 %collective-permute-start.4 = (bf16[1024,256]{1,0:T(8,128)(2,1)}, bf16[1024,256]{1,0:T(8,128)(2,1)S(1)}, u32[]{:S(2)}, u32[]{:S(2)}) collective-permute-start(bf16[1024,256]{1,0:T(8,128)(2,1)} %refs_1_.1), channel_id=1, source_target_pairs={{0,2},{1,3},{2,0},{3,1},{4,6},{5,7},{6,4},{7,5},{8,10},{9,11},{10,... | collective-permute-start | bytes 1572872 | tf_op jit(solution)/shard_map/ppermute | solution.py:460
  3.7 2.7 %shard_map.101 = (f32[8,8,128]{2,1,0:T(8,128)S(1)}, f32[128,64]{1,0:T(8,128)S(1)}, f32[8,64,256]{2,1,0:T(8,128)S(1)}, f32[72,256]{1,0:T(8,128)S(1)}) custom-call(f32[4,1024]{1,0:T(4,128)} %bitcast.2, bf16[1024,256]{1,0:T(8,128)(2,1)} %key.5, bf16[1024,256]{1,0:T(8,128)(2,1)} %value.7), custom_call_target="tpu_custom_call" | custom-call | flops 3000000000 | tf_op jit(solution)/shard_map/pallas_call | solution.py:444
  6.4 1.6 %collective-permute-start.6 = (f32[72,256]{1,0:T(8,128)S(1)}, f32[72,256]{1,0:T(8,128)S(1)}, u32[]{:S(2)}, u32[]{:S(2)}) collective-permute-start(f32[72,256]{1,0:T(8,128)S(1)} %get-tuple-element.43.mine), channel_id=1, source_target_pairs={{0,4},{4,0},{8,12},{12,8},{1,5},{5,1},{9,13},{13,9},{2,6},{6,2},{1... | collective-permute-start | bytes 221192 | tf_op jit(solution)/shard_map/ppermute | solution.py:460
  8.0 0.4 collective-permute-start
  8.5 2.6 %collective-permute-start.1 = (bf16[256,256]{1,0:T(8,128)(2,1)S(1)}, bf16[256,256]{1,0:T(8,128)(2,1)S(1)}, u32[]{:S(2)}, u32[]{:S(2)}) collective-permute-start(bf16[256,256]{1,0:T(8,128)(2,1)S(1)} %copy-done.4), channel_id=1, source_target_pairs={{0,8},{4,12},{8,0},{12,4},{16,28},{20,24},{24,20},{28,16},{1,9},{5... | collective-permute-start | bytes 393224 | tf_op jit(solution)/shard_map/ppermute | solution.py:489
  11.1 1.9 %collective-permute-done.6.other = f32[72,256]{1,0:T(8,128)S(1)} collective-permute-done((f32[72,256]{1,0:T(8,128)S(1)}, f32[72,256]{1,0:T(8,128)S(1)}, u32[]{:S(2)}, u32[]{:S(2)}) %collective-permute-start.6) | collective-permute-done | bytes 73760 | tf_op jit(solution)/shard_map/ppermute | solution.py:460
  13.0 1.2 %collective-permute-start.7 = (f32[72,256]{1,0:T(8,128)S(1)}, f32[72,256]{1,0:T(8,128)S(1)}, u32[]{:S(2)}, u32[]{:S(2)}) collective-permute-start(f32[72,256]{1,0:T(8,128)S(1)} %get-tuple-element.45), channel_id=1, source_target_pairs={{0,8},{4,12},{8,0},{12,4},{1,9},{5,13},{9,1},{13,5},{2,10},{6,14},... | collective-permute-start | bytes 221192 | tf_op jit(solution)/shard_map/ppermute | solution.py:460
  14.3 1.5 %collective-permute-done.4.refs_6_.refs_3_ = bf16[1024,256]{1,0:T(8,128)(2,1)S(1)} collective-permute-done((bf16[1024,256]{1,0:T(8,128)(2,1)}, bf16[1024,256]{1,0:T(8,128)(2,1)S(1)}, u32[]{:S(2)}, u32[]{:S(2)}) %collective-permute-start.4) | collective-permute-done | bytes 524320 | tf_op jit(solution)/shard_map/ppermute | solution.py:460
  15.8 1.8 %shard_map.103 = (f32[1024,256]{1,0:T(8,128)S(1)}, f32[1024,512]{1,0:T(8,128)S(1)}, f32[1024,512]{1,0:T(8,128)S(1)}, bf16[1024,512]{1,0:T(8,128)(2,1)S(1)}, bf16[1024,512]{1,0:T(8,128)(2,1)S(1)}) custom-call(bf16[1024,256]{1,0:T(8,128)(2,1)S(1)} %copy-done.1, bf16[1024,256]{1,0:T(8,128)(2,1)S(1)} %copy-done.2, bf16[1024,256]{1,0:T(8,128)(2,1)S(1)} %copy-done.3, ...), custom_call_target="tpu_custom_call" | custom-call | flops 4000000000 | tf_op jit(solution)/shard_map/pallas_call | solution.py:444
  17.7 3.0 %collective-permute-start.2 = (bf16[256,256]{1,0:T(8,128)(2,1)S(1)}, bf16[256,256]{1,0:T(8,128)(2,1)S(1)}, u32[]{:S(2)}, u32[]{:S(2)}) collective-permute-start(bf16[256,256]{1,0:T(8,128)(2,1)S(1)} %collective-permute-done.1.refs_2_), channel_id=1, source_target_pairs={{0,16},{16,0},{1,17},{17,1},{2,18},{18,2},{3,19},{19,3},{4,20},{20... | collective-permute-start | bytes 393224 | tf_op jit(solution)/shard_map/ppermute | solution.py:460
  20.8 1.5 %shard_map.105 = (bf16[256,1024]{1,0:T(8,128)(2,1)S(1)}, f32[9,64,256]{2,1,0:T(8,128)S(1)}) custom-call(bf16[1024,256]{1,0:T(8,128)(2,1)S(1)} %copy-done.1, f32[128,64]{1,0:T(8,128)S(1)} %get-tuple-element.38.refs_9_.ccol, f32[1024,256]{1,0:T(8,128)S(1)} %get-tuple-element.42.inside, f32[72,256]{1,0:T(8,128)S(1)} %get-tuple-element.44.before, ...), custom_call_target="tpu_custom_call" | custom-call | flops 3000000000 | tf_op jit(solution)/shard_map/pallas_call | solution.py:444
  22.3 1.3 %collective-permute-done.2.refs_3_ = bf16[256,256]{1,0:T(8,128)(2,1)S(1)} collective-permute-done((bf16[256,256]{1,0:T(8,128)(2,1)S(1)}, bf16[256,256]{1,0:T(8,128)(2,1)S(1)}, u32[]{:S(2)}, u32[]{:S(2)}) %collective-permute-start.2) | collective-permute-done | bytes 131104 | tf_op jit(solution)/shard_map/ppermute | solution.py:460
  23.7 1.7 %shard_map.102 = (bf16[1024,256]{1,0:T(8,128)(2,1)S(1)}, bf16[1024,256]{1,0:T(8,128)(2,1)S(1)}, f32[8,64,256]{2,1,0:T(8,128)S(1)}, f32[72,256]{1,0:T(8,128)S(1)}) custom-call(bf16[256,256]{1,0:T(8,128)(2,1)S(1)} %copy-done.4, bf16[256,256]{1,0:T(8,128)(2,1)S(1)} %collective-permute-done.refs_1_, bf16[256,256]{1,0:T(8,128)(2,1)S(1)} %collective-permute-done.1.refs_2_, ...), custom_call_target="tpu_custom_call" | custom-call | flops 3000000000 | tf_op jit(solution)/shard_map/pallas_call | solution.py:444
  25.4 1.9 %collective-permute-start.8 = (f32[72,256]{1,0:T(8,128)S(1)}, f32[72,256]{1,0:T(8,128)S(1)}, u32[]{:S(2)}, u32[]{:S(2)}) collective-permute-start(f32[72,256]{1,0:T(8,128)S(1)} %get-tuple-element.55.mine), channel_id=1, source_target_pairs={{0,4},{4,0},{8,12},{12,8},{1,5},{5,1},{9,13},{13,9},{2,6},{6,2},{1... | collective-permute-start | bytes 221192 | tf_op jit(solution)/shard_map/ppermute | solution.py:460
  27.3 0.8 %shard_map.109 = (f32[256,256]{1,0:T(8,128)S(1)}, bf16[256,256]{1,0:T(8,128)(2,1)S(1)}, bf16[256,256]{1,0:T(8,128)(2,1)S(1)}, bf16[256,256]{1,0:T(8,128)(2,1)S(1)}) custom-call(bf16[256,1024]{1,0:T(8,128)(2,1)S(1)} %get-tuple-element.62.refs_0_, bf16[1024,256]{1,0:T(8,128)(2,1)S(1)} %copy-done, bf16[1024,256]{1,0:T(8,128)(2,1)S(1)} %collective-permute-done.3.refs_5_.refs_2_, ...), custom_call_target="tpu_custom_call" | custom-call | flops 2000000000 | tf_op jit(solution)/shard_map/pallas_call | solution.py:444
  28.1 0.3 collective-permute-start.10
  28.4 2.8 %collective-permute-start.11 = (bf16[256,256]{1,0:T(8,128)(2,1)S(1)}, bf16[256,256]{1,0:T(8,128)(2,1)S(1)}, u32[]{:S(2)}, u32[]{:S(2)}) collective-permute-start(bf16[256,256]{1,0:T(8,128)(2,1)S(1)} %get-tuple-element.65), channel_id=1, source_target_pairs={{0,8},{4,12},{8,0},{12,4},{1,9},{5,13},{9,1},{13,5},{2,10},{6,14},... | collective-permute-start | bytes 393224 | tf_op jit(solution)/shard_map/ppermute | solution.py:460
  31.2 1.4 %collective-permute-start.12 = (bf16[256,256]{1,0:T(8,128)(2,1)S(1)}, bf16[256,256]{1,0:T(8,128)(2,1)S(1)}, u32[]{:S(2)}, u32[]{:S(2)}) collective-permute-start(bf16[256,256]{1,0:T(8,128)(2,1)S(1)} %get-tuple-element.66), channel_id=1, source_target_pairs={{0,12},{4,8},{8,4},{12,0},{1,13},{5,9},{9,5},{13,1},{2,14},{6,10},... | collective-permute-start | bytes 393224 | tf_op jit(solution)/shard_map/ppermute | solution.py:460
  32.5 3.8 %shard_map.106 = (bf16[1024,256]{1,0:T(8,128)(2,1)}, f32[128,64]{1,0:T(8,128)S(1)}) custom-call(bf16[1024,256]{1,0:T(8,128)(2,1)S(1)} %copy-done.1, bf16[1024,256]{1,0:T(8,128)(2,1)S(1)} %copy-done.2, bf16[1024,256]{1,0:T(8,128)(2,1)S(1)} %copy-done.3, bf16[1024,256]{1,0:T(8,128)(2,1)S(1)} %get-tuple-element.39.grad_high, ...), custom_call_target="tpu_custom_call" | custom-call | flops 4000000000 | tf_op jit(solution)/shard_map/pallas_call | solution.py:444
  36.3 1.8 %collective-permute-start.9 = (f32[72,256]{1,0:T(8,128)S(1)}, f32[72,256]{1,0:T(8,128)S(1)}, u32[]{:S(2)}, u32[]{:S(2)}) collective-permute-start(f32[72,256]{1,0:T(8,128)S(1)} %get-tuple-element.57), channel_id=1, source_target_pairs={{0,8},{4,12},{8,0},{12,4},{1,9},{5,13},{9,1},{13,5},{2,10},{6,14},... | collective-permute-start | bytes 221192 | tf_op jit(solution)/shard_map/ppermute | solution.py:460
  38.1 1.9 %shard_map.107 = (f32[1024,256]{1,0:T(8,128)S(1)}, f32[1024,256]{1,0:T(8,128)S(1)}, f32[1024,256]{1,0:T(8,128)S(1)}, f32[8,8,256]{2,1,0:T(8,128)S(1)}) custom-call(bf16[1024,256]{1,0:T(8,128)(2,1)S(1)} %copy-done.1, bf16[1024,256]{1,0:T(8,128)(2,1)S(1)} %copy-done.3, bf16[1024,256]{1,0:T(8,128)(2,1)S(1)} %get-tuple-element.39.grad_high, ...), custom_call_target="tpu_custom_call" | custom-call | flops 4000000000 | tf_op jit(solution)/shard_map/pallas_call | solution.py:444
  40.1 2.8 %collective-permute-done.11.rest_2_ = bf16[256,256]{1,0:T(8,128)(2,1)S(1)} collective-permute-done((bf16[256,256]{1,0:T(8,128)(2,1)S(1)}, bf16[256,256]{1,0:T(8,128)(2,1)S(1)}, u32[]{:S(2)}, u32[]{:S(2)}) %collective-permute-start.11) | collective-permute-done | bytes 131104 | tf_op jit(solution)/shard_map/ppermute | solution.py:460
  42.8 2.8 %collective-permute-done.9.other = f32[72,256]{1,0:T(8,128)S(1)} collective-permute-done((f32[72,256]{1,0:T(8,128)S(1)}, f32[72,256]{1,0:T(8,128)S(1)}, u32[]{:S(2)}, u32[]{:S(2)}) %collective-permute-start.9) | collective-permute-done | bytes 73760 | tf_op jit(solution)/shard_map/ppermute | solution.py:460
  45.6 2.4 %shard_map.110 = (bf16[1024,256]{1,0:T(8,128)(2,1)}, bf16[1024,256]{1,0:T(8,128)(2,1)}, f32[4,1024]{1,0:T(4,128)}, f32[256,256]{1,0:T(8,128)}) custom-call(bf16[1024,256]{1,0:T(8,128)(2,1)S(1)} %copy-done.2, bf16[1024,256]{1,0:T(8,128)(2,1)S(1)} %copy-done.3, f32[1024,256]{1,0:T(8,128)S(1)} %get-tuple-element.53.shrinks, ...), custom_call_target="tpu_custom_call" | custom-call | flops 4000000000 | tf_op jit(solution)/shard_map/pallas_call | solution.py:444
  (22 shorter events, 0.2 us)
Async XLA Ops:
  0.6 15.2 %collective-permute-start.4 = (bf16[1024,256]{1,0:T(8,128)(2,1)}, bf16[1024,256]{1,0:T(8,128)(2,1)S(1)}, u32[]{:S(2)}, u32[]{:S(2)}) collective-permute-start(bf16[1024,256]{1,0:T(8,128)(2,1)} %refs_1_.1), channel_id=1, source_target_pairs={{0,2},{1,3},{2,0},{3,1},{4,6},{5,7},{6,4},{7,5},{8,10},{9,11},{10,... | collective-permute-start | bytes 1572872 | tf_op jit(solution)/shard_map/ppermute | solution.py:460
  3.7 4.3 %copy-start.4 = (bf16[256,256]{1,0:T(8,128)(2,1)S(1)}, bf16[256,256]{1,0:T(8,128)(2,1)}, u32[]{:S(2)}) copy-start(bf16[256,256]{1,0:T(8,128)(2,1)} %refs_0_.1) | copy-start | bytes 393220
  3.7 7.4 %copy-start = (bf16[1024,256]{1,0:T(8,128)(2,1)S(1)}, bf16[1024,256]{1,0:T(8,128)(2,1)}, u32[]{:S(2)}) copy-start(bf16[1024,256]{1,0:T(8,128)(2,1)} %refs_1_.1) | copy-start | bytes 1572868
  6.3 9.5 %copy-start.1 = (bf16[1024,256]{1,0:T(8,128)(2,1)S(1)}, bf16[1024,256]{1,0:T(8,128)(2,1)}, u32[]{:S(2)}) copy-start(bf16[1024,256]{1,0:T(8,128)(2,1)} %query.7) | copy-start | bytes 1572868
  6.3 9.5 %copy-start.2 = (bf16[1024,256]{1,0:T(8,128)(2,1)S(1)}, bf16[1024,256]{1,0:T(8,128)(2,1)}, u32[]{:S(2)}) copy-start(bf16[1024,256]{1,0:T(8,128)(2,1)} %key.5) | copy-start | bytes 1572868
  6.4 9.5 %copy-start.3 = (bf16[1024,256]{1,0:T(8,128)(2,1)S(1)}, bf16[1024,256]{1,0:T(8,128)(2,1)}, u32[]{:S(2)}) copy-start(bf16[1024,256]{1,0:T(8,128)(2,1)} %value.7) | copy-start | bytes 1572868
  6.4 6.6 %collective-permute-start.6 = (f32[72,256]{1,0:T(8,128)S(1)}, f32[72,256]{1,0:T(8,128)S(1)}, u32[]{:S(2)}, u32[]{:S(2)}) collective-permute-start(f32[72,256]{1,0:T(8,128)S(1)} %get-tuple-element.43.mine), channel_id=1, source_target_pairs={{0,4},{4,0},{8,12},{12,8},{1,5},{5,1},{9,13},{13,9},{2,6},{6,2},{1... | collective-permute-start | bytes 221192 | tf_op jit(solution)/shard_map/ppermute | solution.py:460
  8.0 14.3 %collective-permute-start = (bf16[256,256]{1,0:T(8,128)(2,1)S(1)}, bf16[256,256]{1,0:T(8,128)(2,1)S(1)}, u32[]{:S(2)}, u32[]{:S(2)}) collective-permute-start(bf16[256,256]{1,0:T(8,128)(2,1)S(1)} %copy-done.4), channel_id=1, source_target_pairs={{0,4},{4,0},{8,12},{12,8},{1,5},{5,1},{9,13},{13,9},{2,6},{6,2},{1... | collective-permute-start | bytes 393224 | tf_op jit(solution)/shard_map/ppermute | solution.py:460
  8.5 9.2 %collective-permute-start.1 = (bf16[256,256]{1,0:T(8,128)(2,1)S(1)}, bf16[256,256]{1,0:T(8,128)(2,1)S(1)}, u32[]{:S(2)}, u32[]{:S(2)}) collective-permute-start(bf16[256,256]{1,0:T(8,128)(2,1)S(1)} %copy-done.4), channel_id=1, source_target_pairs={{0,8},{4,12},{8,0},{12,4},{16,28},{20,24},{24,20},{28,16},{1,9},{5... | collective-permute-start | bytes 393224 | tf_op jit(solution)/shard_map/ppermute | solution.py:489
  11.1 12.6 %collective-permute-start.3 = (bf16[1024,256]{1,0:T(8,128)(2,1)S(1)}, bf16[1024,256]{1,0:T(8,128)(2,1)S(1)}, u32[]{:S(2)}, u32[]{:S(2)}) collective-permute-start(bf16[1024,256]{1,0:T(8,128)(2,1)S(1)} %copy-done), channel_id=1, source_target_pairs={{0,1},{1,0},{2,3},{3,2},{4,5},{5,4},{6,7},{7,6},{8,9},{9,8},{10,11... | collective-permute-start | bytes 1572872 | tf_op jit(solution)/shard_map/ppermute | solution.py:460
  13.0 7.8 %collective-permute-start.7 = (f32[72,256]{1,0:T(8,128)S(1)}, f32[72,256]{1,0:T(8,128)S(1)}, u32[]{:S(2)}, u32[]{:S(2)}) collective-permute-start(f32[72,256]{1,0:T(8,128)S(1)} %get-tuple-element.45), channel_id=1, source_target_pairs={{0,8},{4,12},{8,0},{12,4},{1,9},{5,13},{9,1},{13,5},{2,10},{6,14},... | collective-permute-start | bytes 221192 | tf_op jit(solution)/shard_map/ppermute | solution.py:460
  15.8 7.9 %collective-permute-start.5 = (bf16[1024,256]{1,0:T(8,128)(2,1)S(1)}, bf16[1024,256]{1,0:T(8,128)(2,1)S(1)}, u32[]{:S(2)}, u32[]{:S(2)}) collective-permute-start(bf16[1024,256]{1,0:T(8,128)(2,1)S(1)} %collective-permute-done.4.refs_6_.refs_3_), channel_id=1, source_target_pairs={{0,1},{1,0},{2,3},{3,2},{4,5},{5,4},{6,7},{7,6},{8,9},{9,8},{10,11... | collective-permute-start | bytes 1572872 | tf_op jit(solution)/shard_map/ppermute | solution.py:460
  17.7 6.0 %collective-permute-start.2 = (bf16[256,256]{1,0:T(8,128)(2,1)S(1)}, bf16[256,256]{1,0:T(8,128)(2,1)S(1)}, u32[]{:S(2)}, u32[]{:S(2)}) collective-permute-start(bf16[256,256]{1,0:T(8,128)(2,1)S(1)} %collective-permute-done.1.refs_2_), channel_id=1, source_target_pairs={{0,16},{16,0},{1,17},{17,1},{2,18},{18,2},{3,19},{19,3},{4,20},{20... | collective-permute-start | bytes 393224 | tf_op jit(solution)/shard_map/ppermute | solution.py:460
  25.4 10.9 %collective-permute-start.8 = (f32[72,256]{1,0:T(8,128)S(1)}, f32[72,256]{1,0:T(8,128)S(1)}, u32[]{:S(2)}, u32[]{:S(2)}) collective-permute-start(f32[72,256]{1,0:T(8,128)S(1)} %get-tuple-element.55.mine), channel_id=1, source_target_pairs={{0,4},{4,0},{8,12},{12,8},{1,5},{5,1},{9,13},{13,9},{2,6},{6,2},{1... | collective-permute-start | bytes 221192 | tf_op jit(solution)/shard_map/ppermute | solution.py:460
  28.1 12.0 %collective-permute-start.10 = (bf16[256,256]{1,0:T(8,128)(2,1)S(1)}, bf16[256,256]{1,0:T(8,128)(2,1)S(1)}, u32[]{:S(2)}, u32[]{:S(2)}) collective-permute-start(bf16[256,256]{1,0:T(8,128)(2,1)S(1)} %get-tuple-element.64), channel_id=1, source_target_pairs={{0,4},{4,0},{8,12},{12,8},{1,5},{5,1},{9,13},{13,9},{2,6},{6,2},{1... | collective-permute-start | bytes 393224 | tf_op jit(solution)/shard_map/ppermute | solution.py:460
  28.4 14.5 %collective-permute-start.11 = (bf16[256,256]{1,0:T(8,128)(2,1)S(1)}, bf16[256,256]{1,0:T(8,128)(2,1)S(1)}, u32[]{:S(2)}, u32[]{:S(2)}) collective-permute-start(bf16[256,256]{1,0:T(8,128)(2,1)S(1)} %get-tuple-element.65), channel_id=1, source_target_pairs={{0,8},{4,12},{8,0},{12,4},{1,9},{5,13},{9,1},{13,5},{2,10},{6,14},... | collective-permute-start | bytes 393224 | tf_op jit(solution)/shard_map/ppermute | solution.py:460
  31.2 11.7 %collective-permute-start.12 = (bf16[256,256]{1,0:T(8,128)(2,1)S(1)}, bf16[256,256]{1,0:T(8,128)(2,1)S(1)}, u32[]{:S(2)}, u32[]{:S(2)}) collective-permute-start(bf16[256,256]{1,0:T(8,128)(2,1)S(1)} %get-tuple-element.66), channel_id=1, source_target_pairs={{0,12},{4,8},{8,4},{12,0},{1,13},{5,9},{9,5},{13,1},{2,14},{6,10},... | collective-permute-start | bytes 393224 | tf_op jit(solution)/shard_map/ppermute | solution.py:460
  36.3 9.3 %collective-permute-start.9 = (f32[72,256]{1,0:T(8,128)S(1)}, f32[72,256]{1,0:T(8,128)S(1)}, u32[]{:S(2)}, u32[]{:S(2)}) collective-permute-start(f32[72,256]{1,0:T(8,128)S(1)} %get-tuple-element.57), channel_id=1, source_target_pairs={{0,8},{4,12},{8,0},{12,4},{1,9},{5,13},{9,1},{13,5},{2,10},{6,14},... | collective-permute-start | bytes 221192 | tf_op jit(solution)/shard_map/ppermute | solution.py:460
